TPU v7x, 512 devices: a whole 4x4x16 slice. The times are simulated.
512 devices in a mesh: rows: 64 (over x, z), cols: 8 (over y, core).
Axes of the slice: x: 4, y: 4, z: 16, core: 2. Of those that a mesh axis runs over, the one named last changes fastest.
Arguments:
- sketch: bfloat16 [131072, 256], P(('rows', 'cols')), may hold values from -6 to 6
- blocks: bfloat16 [4096, 256, 256], P(('rows', 'cols')), may hold values from -0.375 to 0.375
- block_rows: int32 [4096], P(('rows', 'cols')), may hold values from 0 to 3, as said below
- block_cols: int32 [4096], P(('rows', 'cols')), may hold values from 0 to 63
- counts: int32 [512], P(('rows', 'cols')), may hold values from 1 to 8, as said below
Outputs:
- basis: float32 [65536, 256], P(('rows', 'cols'))
- factor: float32 [256, 256], replicated
Inputs may be any that keep to these rules, and one draw needn't show every extreme that they name: Within one device's 8 slots the pairs (block_rows, block_cols) are distinct. `counts`: some device has exactly 8 live slots.
All inputs are finite; a program needn't handle non-finite values.
Results may differ from a plain program's by a relative error of at most 0.0003.
Values may be sent and summed in bfloat16 or wider, within the bound.
A program may use at most 64 MiB of HBM per device.

v0:
```python
import jax
import jax.numpy as jnp
from jax import lax
from jax.sharding import PartitionSpec as P

RB = 4


def local(sketch, blocks, block_rows, block_cols, counts):
    highest = lax.Precision.HIGHEST
    slots, width, _ = blocks.shape
    columns = sketch.shape[1]
    live_count = counts[0]
    starts = block_cols * width
    panel = lax.all_gather(sketch, "rows", axis=0, tiled=True)
    chosen = jax.vmap(lambda offset: lax.dynamic_slice_in_dim(panel, offset, width, 0))(starts)
    products = jnp.einsum("bij,bjk->bik", blocks, chosen, preferred_element_type=jnp.float32)
    selector = (
        (block_rows[:, None] == jnp.arange(RB, dtype=jnp.int32)[None, :])
        & (jnp.arange(slots, dtype=jnp.int32) < live_count)[:, None]
    ).astype(jnp.float32)
    partial_rows = jnp.einsum("br,bik->rik", selector, products, precision=highest)
    partial_rows = partial_rows.reshape(RB * width, columns)
    total_rows = RB * width * lax.axis_size("rows")
    slab_total = lax.psum(partial_rows, "cols")
    gram_matrix = lax.psum(jnp.dot(slab_total.T, slab_total, precision=highest), "rows")
    share_rows = slab_total.shape[0] // lax.axis_size("cols")
    own_rows = lax.dynamic_slice_in_dim(
        slab_total, lax.axis_index("cols") * share_rows, share_rows, 0
    )
    lower_factor = jnp.linalg.cholesky(gram_matrix)
    root_rows = jnp.sqrt(jnp.float32(total_rows))
    solved = lax.linalg.triangular_solve(
        lower_factor, own_rows, left_side=False, lower=True, transpose_a=True
    )
    return (solved * root_rows, lower_factor.T / root_rows)


def solution(mesh):
    in_specs = (
        P(("rows", "cols"), None),
        P(("rows", "cols"), None, None),
        P(("rows", "cols")),
        P(("rows", "cols")),
        P(("rows", "cols")),
    )
    out_specs = (P(("rows", "cols"), None), P())
    return jax.shard_map(local, mesh=mesh, in_specs=in_specs, out_specs=out_specs, check_vma=False)
```

profile of v0, /device:TPU:1, one launch (start us, length us, event | category | flops | bytes accessed | tf_op | source)
XLA Modules:
  0.0 602.0 jit_solution(694707326038857665)
XLA Ops:
  7.2 0.7 all-gather.2.cloned.1.call-update
  8.0 0.7 fusion.16
  9.3 155.1 %all-gather.2.cloned.1.call-done = bf16[16384,256]{1,0:T(8,128)(2,1)} async-done(((bf16[256,256]{1,0:T(8,128)(2,1)}), bf16[16384,256]{1,0:T(8,128)(2,1)}) %all-gather.2.cloned.1.call-update) | async-done | bytes 8388624 | tf_op jit(solution)/shard_map/all_gather | solution.py:15
  164.4 17.0 %while.2 = (s32[]{:T(128)}, bf16[16384,256]{1,0:T(8,128)(2,1)}, s32[8,2]{0,1:T(2,128)S(1)}, bf16[8,256,256]{2,1,0:T(8,128)(2,1)S(1)}, s32[]{:T(128)}) while((s32[]{:T(128)}, bf16[16384,256]{1,0:T(8,128)(2,1)}, s32[8,2]{0,1:T(2,128)S(1)}, bf16[8,256,256]{2,1,0:T(8,128)(2,1)S(1)}, s32[]{:T(128)}) %tuple.41), condition=%wide.while_cond, body=%wide.while_body.sunk | while | flops 2 | bytes 262241 | solution.py:16
  164.5 0.5 slice.69
  165.0 1.5 bitcast_dynamic-update-slice_fusion.4
  166.6 0.1 constant_dynamic-slice_fusion.4
  166.6 0.5 slice.69
  167.1 1.5 bitcast_dynamic-update-slice_fusion.4
  168.8 0.5 slice.69
  169.3 1.5 bitcast_dynamic-update-slice_fusion.4
  170.9 0.5 slice.69
  171.4 1.5 bitcast_dynamic-update-slice_fusion.4
  173.0 0.5 slice.69
  173.5 1.5 bitcast_dynamic-update-slice_fusion.4
  175.2 0.5 slice.69
  175.7 1.5 bitcast_dynamic-update-slice_fusion.4
  177.3 0.5 slice.69
  177.8 1.5 bitcast_dynamic-update-slice_fusion.4
  179.4 0.5 slice.69
  179.9 1.5 bitcast_dynamic-update-slice_fusion.4
  181.5 1.8 fusion.19
  183.3 2.2 copy.16
  185.6 1.1 fusion
  186.6 1.2 copy.11
  187.9 0.2 all-reduce.7.cloned.1.call-start
  188.1 79.3 %all-reduce.5.cloned.1.call-done = f32[1024,256]{1,0:T(8,128)} async-done(((f32[1024,256]{1,0:T(8,128)}), f32[1024,256]{1,0:T(8,128)}) %all-reduce.5.cloned.1.call-update) | async-done | bytes 1048592 | tf_op jit(solution)/shard_map/psum | solution.py:25
  267.4 4.1 fusion.20
  271.5 257.9 %all-reduce.7.cloned.1.call-done = f32[256,256]{0,1:T(8,128)} async-done(((f32[256,256]{0,1:T(8,128)}), f32[256,256]{0,1:T(8,128)}) %all-reduce.7.cloned.1.call-update) | async-done | bytes 262160 | tf_op jit(solution)/shard_map/psum | solution.py:26
  529.4 1.1 copy.13
  530.5 1.0 fusion.2
  531.5 11.7 %cholesky.50 = f32[128,128]{1,0:T(8,128)S(1)} custom-call(f32[128,128]{1,0:T(8,128)S(1)} %cholesky.118), custom_call_target="Cholesky" | custom-call | tf_op jit(solution)/shard_map/jit(cholesky)/cholesky | solution.py:31
  543.3 9.8 %custom-call.14 = f32[1,128,128]{1,2,0:T(8,128)S(1)} custom-call(f32[1,128,128]{2,1,0:T(8,128)S(1)} %get-tuple-element.45), custom_call_target="InvertDiagBlocksLowerTriangular" | custom-call | tf_op jit(solution)/shard_map/jit(cholesky)/cholesky | solution.py:31
  553.1 0.2 constant_dynamic-update-slice_fusion.1
  553.3 0.3 convolution_subtract_fusion.1
  553.6 11.7 %cholesky.105 = f32[128,128]{1,0:T(8,128)S(1)} custom-call(f32[128,128]{1,0:T(8,128)S(1)} %convolution_subtract_fusion.1), custom_call_target="Cholesky" | custom-call | tf_op jit(solution)/shard_map/jit(cholesky)/cholesky | solution.py:31
  565.3 0.8 compare_reduce_fusion
  567.6 4.0 while.3
  567.6 0.6 fusion.30
  568.2 1.4 bitcast_dynamic-update-slice_fusion.5
  569.6 0.6 fusion.30
  570.2 1.4 bitcast_dynamic-update-slice_fusion.5
  571.6 19.7 %custom-call.15 = f32[2,128,128]{1,2,0:T(8,128)S(1)} custom-call(f32[2,128,128]{2,1,0:T(8,128)S(1)} %get-tuple-element.17), custom_call_target="InvertDiagBlocksLowerTriangular" | custom-call | tf_op jit(solution)/shard_map/triangular_solve | solution.py:33
  591.2 1.1 fusion.6
  592.4 1.1 convolution_subtract_fusion
  593.5 0.3 fusion.4
  593.8 0.8 copy.14
  594.6 0.8 copy.15
  (29 shorter events, 0.9 us)
Async XLA Ops:
  7.2 174.3 %copy-start = (bf16[8,256,256]{2,1,0:T(8,128)(2,1)S(1)}, bf16[8,256,256]{2,1,0:T(8,128)(2,1)}, u32[]{:S(2)}) copy-start(bf16[8,256,256]{2,1,0:T(8,128)(2,1)} %param.6) | copy-start | bytes 3145732
  7.2 157.2 %all-gather.2.cloned.1.call-start = ((), (), s32[]{:S(2)}) async-start(), calls=%async_computation | async-start | bytes 8519680 | tf_op jit(solution)/shard_map/all_gather | solution.py:15
  7.9 259.5 %all-reduce.5.cloned.1.call-start = ((), (), s32[]{:S(2)}) async-start(), calls=%async_computation.1 | async-start | bytes 2097152 | tf_op jit(solution)/shard_map/psum | solution.py:25
  183.3 2.2 copy-start.1
  187.9 341.5 %all-reduce.7.cloned.1.call-start = ((), (), s32[]{:S(2)}) async-start(), calls=%async_computation.2 | async-start | bytes 524288 | tf_op jit(solution)/shard_map/psum | solution.py:26
Sparse Core Ops, SparseCore 0:
  10.9 153.4 all-gather.1
  188.0 79.3 all-reduce.4
  271.6 257.7 all-reduce.6
where the time goes:
time: 612 us; the launch traced here: 602 us
  waiting for transfers between devices  493 us (81%)
  other arithmetic  55.5 us (9%)
  local copies, waits for them, and re-layouts  27 us (4%)
  between operations  15.9 us (3%)
  matrix products  10 us (2%)
    psum x1, waiting for transfers between devices, local(): lax.psum(jnp.dot(slab_total.T, slab_total, precision=highest), 'rows')  258 us
    all_gather x1, waiting for transfers between devices, local(): panel = lax.all_gather(sketch, 'rows', axis=0, tiled=True)  155 us
    psum x1, waiting for transfers between devices, local(): slab_total = lax.psum(partial_rows, 'cols')  79.3 us
    another operation x6, other arithmetic, local(): lower_factor = jnp.linalg.cholesky(gram_matrix)  34.2 us
    another operation x2, other arithmetic, local(): lax.linalg.triangular_solve(lower_factor, own_rows, left_side=False, lowe...  19.7 us
    gather x24, local copies, waits for them, and re-layouts  16.9 us
  transfers between devices with their start and end apart: 3, of which 3 were waited for; matrix products, arithmetic and copies ran while one was open for 0% of the time, Pallas kernels for 0%

commit v1 on v0

v1 whole, which is shorter than its diff:
```python
import functools

import jax
import jax.numpy as jnp
from jax import lax
from jax.experimental import pallas as pl
from jax.experimental.pallas import tpu as pltpu
from jax.sharding import PartitionSpec as P

MESH = pl.DeviceIdType.MESH
HIGHEST = lax.Precision.HIGHEST
RB = 4
NX, NZ, NY, NC = 4, 16, 4, 2
WIDTH = 256
SPLIT = 96
GROUP = 32
SHARE = 128


def copy_to(src, dst, send_sem, recv_sem, row, col):
    return pltpu.make_async_remote_copy(
        src_ref=src, dst_ref=dst, send_sem=send_sem, recv_sem=recv_sem,
        device_id=(row, col), device_id_type=MESH,
    )


def greet(peers):
    barrier = pltpu.get_barrier_semaphore()
    for row, col in peers:
        pl.semaphore_signal(barrier, inc=1, device_id=(row, col), device_id_type=MESH)
    pl.semaphore_wait(barrier, len(peers))


def sketch_kernel(
    rows_ref, cols_ref, counts_ref, sketch_ref, blocks_ref, own_ref, gram_ref,
    panel, partial, received, half, received2,
    local_sem, xa_send, xa_recv, za_send, za_recv, zb_send, zb_recv,
    xb_send, xb_recv, op_send, op_recv, c_send, c_recv, y_send, y_recv,
):
    r = lax.axis_index("rows")
    c = lax.axis_index("cols")
    x, z = r // NZ, lax.rem(r, NZ)
    y, core = c // NC, lax.rem(c, NC)

    def at_x(k):
        return lax.rem(x + k, NX) * NZ + z

    def at_z(k):
        return x * NZ + lax.rem(z + k, NZ)

    greet(
        [(at_x(k), c) for k in (1, 2, 3)]
        + [(at_z(1), c), (at_z(NZ - 1), c), (r, y * NC + 1 - core)]
        + [(r, lax.rem(y + k, NY) * NC + core) for k in (1, 2, 3)]
    )

    local = pltpu.make_async_copy(sketch_ref, panel.at[x, z], local_sem)
    local.start()
    local.wait()

    first = pl.ds(0, SPLIT)
    second = pl.ds(SPLIT, WIDTH - SPLIT)

    def shifted(k):
        return lax.rem(z + k + NZ, NZ)

    def xa(k):
        piece = panel.at[x, z, first]
        return copy_to(piece, piece, xa_send.at[k - 1], xa_recv.at[k - 1], at_x(k), c)

    def za(side, hop):
        step = 1 - 2 * side
        piece = panel.at[:, shifted(-step * (hop - 1)), first]
        to = at_z(1 if side == 0 else NZ - 1)
        return copy_to(piece, piece, za_send.at[side, hop - 1], za_recv.at[side, hop - 1], to, c)

    def za_arrived(side, hop):
        step = 1 - 2 * side
        piece = panel.at[:, shifted(-step * hop), first]
        to = at_z(1 if side == 0 else NZ - 1)
        copy_to(piece, piece, za_send.at[side, hop - 1], za_recv.at[side, hop - 1], to, c).wait_recv()

    def zb(side, hop):
        step = 1 - 2 * side
        piece = panel.at[x, shifted(-step * (hop - 1)), second]
        to = at_z(1 if side == 0 else NZ - 1)
        return copy_to(piece, piece, zb_send.at[side, hop - 1], zb_recv.at[side, hop - 1], to, c)

    def zb_arrived(side, hop):
        step = 1 - 2 * side
        piece = panel.at[x, shifted(-step * hop), second]
        to = at_z(1 if side == 0 else NZ - 1)
        copy_to(piece, piece, zb_send.at[side, hop - 1], zb_recv.at[side, hop - 1], to, c).wait_recv()

    def piece_of(family, slot, column):
        at = shifted(-slot - 1) if family == 0 else shifted(slot)
        return panel.at[column, at, second]

    def xb(family, slot, way):
        piece = piece_of(family, slot, x)
        to = at_x(1 if way == 0 else NX - 1)
        return copy_to(piece, piece, xb_send.at[family, way, slot], xb_recv.at[family, way, slot], to, c)

    def xb_arrived(family, slot, way):
        column = lax.rem(x + (NX - 1 if way == 0 else 1), NX)
        piece = piece_of(family, slot, column)
        to = at_x(1 if way == 0 else NX - 1)
        copy_to(piece, piece, xb_send.at[family, way, slot], xb_recv.at[family, way, slot], to, c).wait_recv()

    def op(family, slot):
        column = lax.rem(x + (NX - 1 if family == 0 else 1), NX)
        piece = piece_of(family, slot, column)
        to = at_x(1 if family == 0 else NX - 1)
        return copy_to(piece, piece, op_send.at[family, slot], op_recv.at[family, slot], to, c)

    def op_arrived(family, slot):
        piece = piece_of(family, slot, lax.rem(x + 2, NX))
        to = at_x(1 if family == 0 else NX - 1)
        copy_to(piece, piece, op_send.at[family, slot], op_recv.at[family, slot], to, c).wait_recv()

    for k in (1, 2, 3):
        xa(k).start()
    for side in (0, 1):
        zb(side, 1).start()
    for way in (0, 1):
        xb(1, 0, way).start()
    for k in (1, 2, 3):
        piece = panel.at[lax.rem(x + NX - k, NX), z, first]
        copy_to(piece, piece, xa_send.at[k - 1], xa_recv.at[k - 1], at_x(k), c).wait_recv()
    for side in (0, 1):
        za(side, 1).start()

    def hop_body(hop, carry):
        zb_arrived(0, hop)
        zb(0, hop + 1).start()
        for way in (0, 1):
            xb(0, hop - 1, way).start()
        zb_arrived(1, hop)

        @pl.when(hop < 7)
        def _():
            zb(1, hop + 1).start()

        for way in (0, 1):
            xb(1, hop, way).start()
        za_arrived(1, hop)
        za(1, hop + 1).start()
        za_arrived(0, hop)

        @pl.when(hop < 7)
        def _():
            za(0, hop + 1).start()

        xb_arrived(1, hop - 1, 1)
        op(1, hop - 1).start()

        @pl.when(hop > 1)
        def _():
            xb_arrived(0, hop - 2, 0)
            op(0, hop - 2).start()

        return carry

    lax.fori_loop(1, 8, hop_body, 0)
    zb_arrived(0, 8)
    for way in (0, 1):
        xb(0, 7, way).start()
    xb_arrived(1, 7, 1)
    op(1, 7).start()
    xb_arrived(0, 6, 0)
    op(0, 6).start()
    xb_arrived(0, 7, 0)
    op(0, 7).start()
    za_arrived(1, 8)

    def drain(slot, carry):
        xb_arrived(0, slot, 1)
        xb_arrived(1, slot, 0)
        for family in (0, 1):
            op_arrived(family, slot)
            op(family, slot).wait_send()
            for way in (0, 1):
                xb(family, slot, way).wait_send()
        zb(0, slot + 1).wait_send()
        za(1, slot + 1).wait_send()

        @pl.when(slot < 7)
        def _():
            zb(1, slot + 1).wait_send()
            za(0, slot + 1).wait_send()

        return carry

    lax.fori_loop(0, 8, drain, 0)
    for k in (1, 2, 3):
        xa(k).wait_send()

    partial[...] = jnp.zeros_like(partial)
    live = counts_ref[0]

    def slot_body(s, carry):
        q = cols_ref[s]
        product = jnp.dot(
            blocks_ref[s], panel[q // NZ, lax.rem(q, NZ)], preferred_element_type=jnp.float32
        )
        for b in range(RB):
            weight = jnp.where(jnp.logical_and(rows_ref[s] == b, s < live), 1.0, 0.0)
            for part in range(NC):
                partial[b, part] += weight * product[part * SHARE:(part + 1) * SHARE]
        return carry

    lax.fori_loop(0, 8, slot_body, 0)

    pair = copy_to(partial.at[:, 1 - core], received, c_send, c_recv, r, y * NC + 1 - core)
    pair.start()
    pair.wait()
    half[...] = partial[:, core] + received[...]
    sends = []
    for k in (1, 2, 3):
        other = lax.rem(y + k, NY)
        send = copy_to(
            half.at[other], received2.at[k - 1], y_send.at[k - 1], y_recv.at[k - 1], r, other * NC + core
        )
        send.start()
        sends.append(send)
    for send in sends:
        send.wait()
    own = half[y] + received2[0] + received2[1] + received2[2]
    own_ref[...] = own
    gram_ref[...] = lax.dot_general(
        own, own, (((0,), (0,)), ((), ())), precision=HIGHEST, preferred_element_type=jnp.float32
    )


def sum_kernel(gram_ref, out_ref, slots, lines, a_send, a_recv, z_send, z_recv, b_send, b_recv):
    r = lax.axis_index("rows")
    c = lax.axis_index("cols")
    x, z = r // NZ, lax.rem(r, NZ)
    cols = NY * NC
    me = x * cols + c

    def member(k):
        other = lax.rem(me + k, GROUP)
        return other, (other // cols) * NZ + z, lax.rem(other, cols)

    def along(k):
        return x * NZ + lax.rem(z + k, NZ)

    barrier = pltpu.get_barrier_semaphore()

    def hello_group(k, carry):
        _, row, col = member(k)
        pl.semaphore_signal(barrier, inc=1, device_id=(row, col), device_id_type=MESH)
        return carry

    def hello_line(k, carry):
        pl.semaphore_signal(barrier, inc=1, device_id=(along(k), c), device_id_type=MESH)
        return carry

    lax.fori_loop(1, GROUP, hello_group, 0)
    lax.fori_loop(1, NZ, hello_line, 0)
    pl.semaphore_wait(barrier, GROUP - 1 + NZ - 1)

    def scatter(k):
        other, row, col = member(k)
        return copy_to(gram_ref.at[other], slots.at[k - 1], a_send.at[k - 1], a_recv.at[k - 1], row, col)

    def line(k):
        return copy_to(lines.at[z], lines.at[z], z_send.at[k - 1], z_recv.at[k - 1], along(k), c)

    def line_arrived(k):
        source = lax.rem(z + NZ - k, NZ)
        copy_to(
            lines.at[source], lines.at[source], z_send.at[k - 1], z_recv.at[k - 1], along(k), c
        ).wait_recv()

    def spread(k):
        _, row, col = member(k)
        return copy_to(out_ref.at[me], out_ref.at[me], b_send.at[k - 1], b_recv.at[k - 1], row, col)

    def spread_arrived(k):
        _, row, col = member(k)
        source = lax.rem(me + GROUP - k, GROUP)
        copy_to(
            out_ref.at[source], out_ref.at[source], b_send.at[k - 1], b_recv.at[k - 1], row, col
        ).wait_recv()

    def loop(start, stop, act):
        def body(k, carry):
            act(k)
            return carry
        lax.fori_loop(start, stop, body, 0)

    loop(1, GROUP, lambda k: scatter(k).start())
    loop(1, GROUP, lambda k: scatter(k).wait())
    lines[z] = gram_ref[me] + jnp.sum(slots[...], axis=0)
    loop(1, NZ, lambda k: line(k).start())
    loop(1, NZ, line_arrived)
    out_ref[me] = jnp.sum(lines[...], axis=0)
    loop(1, GROUP, lambda k: spread(k).start())
    loop(1, GROUP, spread_arrived)
    loop(1, NZ, lambda k: line(k).wait_send())
    loop(1, GROUP, lambda k: spread(k).wait_send())


def local(sketch, blocks, block_rows, block_cols, counts):
    f32 = jnp.float32
    dma = pltpu.SemaphoreType.DMA
    vmem = pl.BlockSpec(memory_space=pltpu.VMEM)
    smem = pl.BlockSpec(memory_space=pltpu.SMEM)
    own, gram = pl.pallas_call(
        sketch_kernel,
        out_shape=(
            jax.ShapeDtypeStruct((SHARE, WIDTH), f32),
            jax.ShapeDtypeStruct((WIDTH, WIDTH), f32),
        ),
        in_specs=[smem, smem, smem, vmem, vmem],
        out_specs=(vmem, vmem),
        scratch_shapes=[
            pltpu.VMEM((NX, NZ, WIDTH, WIDTH), jnp.bfloat16),
            pltpu.VMEM((RB, NC, SHARE, WIDTH), f32),
            pltpu.VMEM((RB, SHARE, WIDTH), f32),
            pltpu.VMEM((RB, SHARE, WIDTH), f32),
            pltpu.VMEM((NY - 1, SHARE, WIDTH), f32),
            dma,
            dma((3,)), dma((3,)),
            dma((2, 8)), dma((2, 8)),
            dma((2, 8)), dma((2, 8)),
            dma((2, 2, 8)), dma((2, 2, 8)),
            dma((2, 8)), dma((2, 8)),
            dma, dma,
            dma((3,)), dma((3,)),
        ],
        compiler_params=pltpu.CompilerParams(collective_id=0, has_side_effects=True),
        name="sketch",
    )(block_rows, block_cols, counts, sketch, blocks)
    gram = pl.pallas_call(
        sum_kernel,
        out_shape=jax.ShapeDtypeStruct((GROUP, 8, WIDTH), f32),
        in_specs=[vmem],
        out_specs=vmem,
        scratch_shapes=[
            pltpu.VMEM((GROUP - 1, 8, WIDTH), f32),
            pltpu.VMEM((NZ, 8, WIDTH), f32),
            dma((GROUP - 1,)), dma((GROUP - 1,)),
            dma((NZ - 1,)), dma((NZ - 1,)),
            dma((GROUP - 1,)), dma((GROUP - 1,)),
        ],
        compiler_params=pltpu.CompilerParams(collective_id=1, has_side_effects=True),
        name="gram_sum",
    )(gram.reshape(GROUP, 8, WIDTH)).reshape(WIDTH, WIDTH)
    lower_factor = jnp.linalg.cholesky(gram)
    root_rows = jnp.sqrt(f32(RB * WIDTH * lax.axis_size("rows")))
    solved = lax.linalg.triangular_solve(
        lower_factor, own, left_side=False, lower=True, transpose_a=True
    )
    return (solved * root_rows, lower_factor.T / root_rows)


def solution(mesh):
    in_specs = (
        P(("rows", "cols"), None),
        P(("rows", "cols"), None, None),
        P(("rows", "cols")),
        P(("rows", "cols")),
        P(("rows", "cols")),
    )
    out_specs = (P(("rows", "cols"), None), P())
    return jax.shard_map(local, mesh=mesh, in_specs=in_specs, out_specs=out_specs, check_vma=False)
```

time: 612 us -> 185 us (0.30); the launches traced: 602 us -> 185 us
  waiting for transfers between devices: 493 us -> 0 us
  Pallas kernels: 0 us -> 120 us
  local copies, waits for them, and re-layouts: 27 us -> 6.9 us
  between operations: 15.9 us -> 2.74 us
  matrix products: 10 us -> 1.33 us
    psum x2 -> x0, waiting for transfers between devices: 337 us -> none  [the longest x1 258 us: local(): lax.psum(jnp.dot(slab_total.T, slab_total, precision=highest), 'rows')]
    all_gather x1 -> x0, waiting for transfers between devices: 155 us -> none  [local(): panel = lax.all_gather(sketch, 'rows', axis=0, tiled=True)]
    pallas_call x0 -> x2, Pallas kernels: none -> 120 us  [the longest x1 87.3 us: local(): pl.pallas_call(sketch_kernel, out_shape=(jax.ShapeDtypeStruct((SHARE, WID...]
    gather x24 -> x0, local copies, waits for them, and re-layouts: 16.9 us -> none
    dot_general x3 -> x0, matrix products: 6.98 us -> none  [the longest x1 4.06 us: local(): jnp.dot(slab_total.T, slab_total, precision=highest)]
  transfers between devices with their start and end apart: 3 -> 0, of which waited for: 3 -> 0; matrix products, arithmetic and copies ran while one was open for 0% -> 0% of each run, Pallas kernels for 0% -> 0%
where the time goes in v1:
time: 185 us
  Pallas kernels  120 us (65%)
  other arithmetic  53.7 us (29%)
  local copies, waits for them, and re-layouts  6.9 us (4%)
  between operations  2.74 us (1%)
    pallas_call x1, Pallas kernels, local(): pl.pallas_call(sketch_kernel, out_shape=(jax.ShapeDtypeStruct((SHARE, WID...  87.3 us
    another operation x6, other arithmetic, local(): lower_factor = jnp.linalg.cholesky(gram)  34 us
    pallas_call x1, Pallas kernels, local(): pl.pallas_call(sum_kernel, out_shape=jax.ShapeDtypeStruct((GROUP, 8, WIDT...  32.4 us
    another operation x2, other arithmetic, local(): lax.linalg.triangular_solve(lower_factor, own, left_side=False, lower=Tru...  19.7 us
    another operation x6, local copies, waits for them, and re-layouts  4.06 us

profile of v1, /device:TPU:1, one launch (start us, length us, event | category | flops | bytes accessed | tf_op | source)
XLA Modules:
  0.0 184.5 jit_solution(17630374832586546562)
XLA Ops:
  1.3 87.3 %sketch.1 = (f32[128,256]{1,0:T(8,128)}, f32[256,256]{1,0:T(8,128)}) custom-call(s32[8]{0:T(128)} %rows_ref.1, s32[8]{0:T(128)} %cols_ref.1, s32[1]{0:T(128)S(6)} %copy.24.counts_ref, bf16[256,256]{1,0:T(8,128)(2,1)} %sketch_ref.1, bf16[8,256,256]{2,1,0:T(8,128)(2,1)} %blocks_ref.1), custom_call_target="tpu_custom_call" | custom-call | tf_op jit(solution)/shard_map/sketch/pallas_call | solution.py:311
  88.6 32.4 %gram_sum.1 = f32[32,8,256]{2,1,0:T(8,128)} custom-call(f32[32,8,256]{2,1,0:T(8,128)} %bitcast.37), custom_call_target="tpu_custom_call" | custom-call | tf_op jit(solution)/shard_map/gram_sum/pallas_call | solution.py:337
  121.0 0.0 copy-start
  121.0 1.1 copy.11
  122.1 0.0 copy-done
  122.2 11.7 %cholesky.50 = f32[128,128]{1,0:T(8,128)S(1)} custom-call(f32[128,128]{1,0:T(8,128)S(1)} %cholesky.118), custom_call_target="Cholesky" | custom-call | tf_op jit(solution)/shard_map/jit(cholesky)/cholesky | solution.py:352
  133.9 9.8 %custom-call.14 = f32[1,128,128]{1,2,0:T(8,128)S(1)} custom-call(f32[1,128,128]{2,1,0:T(8,128)S(1)} %get-tuple-element.33), custom_call_target="InvertDiagBlocksLowerTriangular" | custom-call | tf_op jit(solution)/shard_map/jit(cholesky)/cholesky | solution.py:352
  143.8 0.2 constant_dynamic-update-slice_fusion.1
  144.0 0.3 convolution_subtract_fusion.1
  144.3 11.7 %cholesky.105 = f32[128,128]{1,0:T(8,128)S(1)} custom-call(f32[128,128]{1,0:T(8,128)S(1)} %convolution_subtract_fusion.1), custom_call_target="Cholesky" | custom-call | tf_op jit(solution)/shard_map/jit(cholesky)/cholesky | solution.py:352
  156.0 0.6 compare_reduce_fusion
  158.0 0.1 triangular_solve.58
  158.1 0.0 copy-start.1
  158.1 4.2 %while.1 = (s32[]{:T(128)}, f32[256,256]{1,0:T(8,128)S(1)}, s32[2,2]{1,0:T(2,128)S(1)}, f32[2,128,128]{2,1,0:T(8,128)S(1)}, s32[]{:T(128)}) while((s32[]{:T(128)}, f32[256,256]{1,0:T(8,128)S(1)}, s32[2,2]{1,0:T(2,128)S(1)}, f32[2,128,128]{2,1,0:T(8,128)S(1)}, s32[]{:T(128)}) %tuple.30), condition=%wide.while_cond, body=%wide.while_body.sunk | while | flops 2 | bytes 131181 | solution.py:354
  158.3 0.6 fusion.15
  158.8 1.4 bitcast_dynamic-update-slice_fusion.2
  160.3 0.6 fusion.15
  160.9 1.4 bitcast_dynamic-update-slice_fusion.2
  162.3 19.7 %custom-call.15 = f32[2,128,128]{1,2,0:T(8,128)S(1)} custom-call(f32[2,128,128]{2,1,0:T(8,128)S(1)} %get-tuple-element.13), custom_call_target="InvertDiagBlocksLowerTriangular" | custom-call | tf_op jit(solution)/shard_map/triangular_solve | solution.py:354
  182.0 0.0 copy-done.1
  182.0 0.3 fusion.4
  182.3 0.3 convolution_subtract_fusion
  182.6 0.3 fusion.2
  182.9 0.8 copy.12
  183.7 0.8 copy.13
  (11 shorter events, 0.2 us)
Async XLA Ops:
  121.0 1.2 copy-start
  158.1 23.9 %copy-start.1 = (f32[128,256]{1,0:T(8,128)S(1)}, f32[128,256]{1,0:T(8,128)}, u32[]{:S(2)}) copy-start(f32[128,256]{1,0:T(8,128)} %get-tuple-element.4) | copy-start | bytes 393220

commit v2 on v1

--- a/solution.py
+++ b/solution.py
@@ -15,6 +15,7 @@
 SPLIT = 96
 GROUP = 32
 SHARE = 128
+HALF = 128
 
 
 def copy_to(src, dst, send_sem, recv_sem, row, col):
@@ -301,6 +302,84 @@
     loop(1, GROUP, spread_arrived)
     loop(1, NZ, lambda k: line(k).wait_send())
     loop(1, GROUP, lambda k: spread(k).wait_send())
+
+
+def factor_kernel(step, root, gram_ref, own_ref, basis_ref, factor_ref, work, rows):
+    f32 = jnp.float32
+    lane = lax.broadcasted_iota(jnp.int32, (1, HALF), 1)
+    below = lax.broadcasted_iota(jnp.int32, (HALF, HALF), 0) > lax.broadcasted_iota(
+        jnp.int32, (HALF, HALF), 1
+    )
+    eye = (
+        lax.broadcasted_iota(jnp.int32, (HALF, HALF), 0)
+        == lax.broadcasted_iota(jnp.int32, (HALF, HALF), 1)
+    ).astype(f32)
+
+    def dot(a, b, dims):
+        return lax.dot_general(a, b, (dims, ((), ())), precision=HIGHEST, preferred_element_type=f32)
+
+    def pick(value, j):
+        return jnp.sum(jnp.where(lane == j, value, 0.0), axis=1, keepdims=True)
+
+    def eliminate(block):
+        work[:, :HALF] = block
+        work[:, HALF:] = eye
+
+        def body(i, carry):
+            j = i * step
+            line = [work[pl.ds(j + t, 1), :] for t in range(step)]
+            column = [pick(work[:, :HALF], j + t) for t in range(step)]
+            entry = [[pick(line[t][:, :HALF], j + u) for u in range(step)] for t in range(step)]
+            scaled = []
+            for t in range(step):
+                inverse = 1.0 / entry[t][t]
+                for u in range(t + 1, step):
+                    ratio = entry[t][u] * inverse
+                    line[u] = line[u] - ratio * line[t]
+                    column[u] = column[u] - ratio * column[t]
+                    for v in range(u, step):
+                        entry[u][v] = entry[u][v] - ratio * entry[t][v]
+                scaled.append(line[t] * inverse)
+            total = work[...]
+            for t in range(step):
+                total = total - column[t] * scaled[t]
+            work[...] = total
+            for t in range(step):
+                rows[pl.ds(j + t, 1), :] = line[t] * (1.0 / jnp.sqrt(entry[t][t]))
+            return carry
+
+        lax.fori_loop(0, HALF // step, body, 0)
+        return jnp.where(below, 0.0, rows[:, :HALF]), rows[:, HALF:]
+
+    upper1, inverse1 = eliminate(gram_ref[:HALF, :HALF])
+    cross = dot(inverse1, gram_ref[:HALF, HALF:], ((1,), (0,)))
+    factor_ref[:HALF, :HALF] = upper1 * (1.0 / root)
+    factor_ref[:HALF, HALF:] = cross * (1.0 / root)
+    factor_ref[HALF:, :HALF] = jnp.zeros((HALF, HALF), f32)
+    solved = dot(own_ref[:, :HALF], inverse1, ((1,), (1,)))
+    basis_ref[:, :HALF] = solved * root
+    rest = own_ref[:, HALF:] - dot(solved, cross, ((1,), (0,)))
+    schur = gram_ref[HALF:, HALF:] - dot(cross, cross, ((0,), (0,)))
+    upper2, inverse2 = eliminate(schur)
+    factor_ref[HALF:, HALF:] = upper2 * (1.0 / root)
+    basis_ref[:, HALF:] = dot(rest, inverse2, ((1,), (1,))) * root
+
+
+def factorize(gram, own, step):
+    root = float(RB * WIDTH * NX * NZ) ** 0.5
+    f32 = jnp.float32
+    vmem = pl.BlockSpec(memory_space=pltpu.VMEM)
+    return pl.pallas_call(
+        functools.partial(factor_kernel, step, root),
+        out_shape=(
+            jax.ShapeDtypeStruct((SHARE, WIDTH), f32),
+            jax.ShapeDtypeStruct((WIDTH, WIDTH), f32),
+        ),
+        in_specs=[vmem, vmem],
+        out_specs=(vmem, vmem),
+        scratch_shapes=[pltpu.VMEM((HALF, WIDTH), f32), pltpu.VMEM((HALF, WIDTH), f32)],
+        name="factorize",
+    )(gram, own)
 
 
 def local(sketch, blocks, block_rows, block_cols, counts):
@@ -349,12 +428,7 @@
         compiler_params=pltpu.CompilerParams(collective_id=1, has_side_effects=True),
         name="gram_sum",
     )(gram.reshape(GROUP, 8, WIDTH)).reshape(WIDTH, WIDTH)
-    lower_factor = jnp.linalg.cholesky(gram)
-    root_rows = jnp.sqrt(f32(RB * WIDTH * lax.axis_size("rows")))
-    solved = lax.linalg.triangular_solve(
-        lower_factor, own, left_side=False, lower=True, transpose_a=True
-    )
-    return (solved * root_rows, lower_factor.T / root_rows)
+    return factorize(gram, own, 4)
 
 
 def solution(mesh):

time: 185 us -> 135 us (0.73)
  other arithmetic: 53.7 us -> 0 us
  Pallas kernels: 120 us -> 133 us
  local copies, waits for them, and re-layouts: 6.9 us -> 0 us
    another operation x8 -> x0, other arithmetic: 53.6 us -> none  [the longest x6 34 us: local(): lower_factor = jnp.linalg.cholesky(gram)]
    pallas_call x0 -> x1, Pallas kernels: none -> 13.8 us  [factorize(): pl.pallas_call(functools.partial(factor_kernel, step, root), out_shape=(j...]
    another operation x9 -> x0, local copies, waits for them, and re-layouts: 4.15 us -> none
where the time goes in v2:
time: 135 us
  Pallas kernels  133 us (99%)
    pallas_call x1, Pallas kernels, local(): pl.pallas_call(sketch_kernel, out_shape=(jax.ShapeDtypeStruct((SHARE, WID...  87.3 us
    pallas_call x1, Pallas kernels, local(): pl.pallas_call(sum_kernel, out_shape=jax.ShapeDtypeStruct((GROUP, 8, WIDT...  32.4 us
    pallas_call x1, Pallas kernels, factorize(): pl.pallas_call(functools.partial(factor_kernel, step, root), out_shape=(j...  13.8 us

profile of v2, /device:TPU:1, one launch (start us, length us, event | category | flops | bytes accessed | tf_op | source)
XLA Modules:
  0.0 134.7 jit_solution(15610023272082626291)
XLA Ops:
  1.3 87.3 %sketch.1 = (f32[128,256]{1,0:T(8,128)}, f32[256,256]{1,0:T(8,128)}) custom-call(s32[8]{0:T(128)} %rows_ref.1, s32[8]{0:T(128)} %cols_ref.1, s32[1]{0:T(128)S(6)} %copy.7.counts_ref, bf16[256,256]{1,0:T(8,128)(2,1)} %sketch_ref.1, bf16[8,256,256]{2,1,0:T(8,128)(2,1)} %blocks_ref.1), custom_call_target="tpu_custom_call" | custom-call | tf_op jit(solution)/shard_map/sketch/pallas_call | solution.py:390
  88.6 32.4 %gram_sum.1 = f32[32,8,256]{2,1,0:T(8,128)} custom-call(f32[32,8,256]{2,1,0:T(8,128)} %bitcast.3), custom_call_target="tpu_custom_call" | custom-call | tf_op jit(solution)/shard_map/gram_sum/pallas_call | solution.py:416
  121.0 13.8 %factorize.1 = (f32[128,256]{1,0:T(8,128)}, f32[256,256]{1,0:T(8,128)}) custom-call(f32[256,256]{1,0:T(8,128)} %bitcast.2, f32[128,256]{1,0:T(8,128)} %get-tuple-element.5.own_ref), custom_call_target="tpu_custom_call" | custom-call | tf_op jit(solution)/shard_map/factorize/pallas_call | solution.py:372

commit v3 on v2

--- a/solution.py
+++ b/solution.py
@@ -12,8 +12,8 @@
 RB = 4
 NX, NZ, NY, NC = 4, 16, 4, 2
 WIDTH = 256
-SPLIT = 96
-GROUP = 32
+SPLIT = 80
+GROUP, LINE = 32, 4
 SHARE = 128
 HALF = 128
 
@@ -25,18 +25,12 @@
     )
 
 
-def greet(peers):
-    barrier = pltpu.get_barrier_semaphore()
-    for row, col in peers:
-        pl.semaphore_signal(barrier, inc=1, device_id=(row, col), device_id_type=MESH)
-    pl.semaphore_wait(barrier, len(peers))
-
-
 def sketch_kernel(
     rows_ref, cols_ref, counts_ref, sketch_ref, blocks_ref, own_ref, gram_ref,
-    panel, partial, received, half, received2,
+    panel, products, partial, received, half, received2, gram, slots, lows, highs,
     local_sem, xa_send, xa_recv, za_send, za_recv, zb_send, zb_recv,
     xb_send, xb_recv, op_send, op_recv, c_send, c_recv, y_send, y_recv,
+    g_send, g_recv, l_send, l_recv, h_send, h_recv, s_send, s_recv,
 ):
     r = lax.axis_index("rows")
     c = lax.axis_index("cols")
@@ -49,11 +43,37 @@
     def at_z(k):
         return x * NZ + lax.rem(z + k, NZ)
 
-    greet(
-        [(at_x(k), c) for k in (1, 2, 3)]
-        + [(at_z(1), c), (at_z(NZ - 1), c), (r, y * NC + 1 - core)]
-        + [(r, lax.rem(y + k, NY) * NC + core) for k in (1, 2, 3)]
-    )
+    cols = NY * NC
+    me = x * cols + c
+    low, high = lax.rem(z, LINE), z // LINE
+
+    def member(k):
+        other = lax.rem(me + k, GROUP)
+        return other, (other // cols) * NZ + z, lax.rem(other, cols)
+
+    def at_low(k):
+        return x * NZ + high * LINE + lax.rem(low + k, LINE)
+
+    def at_high(k):
+        return x * NZ + lax.rem(high + k, LINE) * LINE + low
+
+    barrier = pltpu.get_barrier_semaphore()
+
+    def hello(row, col):
+        pl.semaphore_signal(barrier, inc=1, device_id=(row, col), device_id_type=MESH)
+
+    def hello_group(k, carry):
+        _, row, col = member(k)
+        hello(row, col)
+        return carry
+
+    for row in (at_z(1), at_z(NZ - 1)):
+        hello(row, c)
+    for k in range(1, LINE):
+        hello(at_low(k), c)
+        hello(at_high(k), c)
+    lax.fori_loop(1, GROUP, hello_group, 0)
+    pl.semaphore_wait(barrier, 2 + 2 * (LINE - 1) + GROUP - 1)
 
     local = pltpu.make_async_copy(sketch_ref, panel.at[x, z], local_sem)
     local.start()
@@ -196,112 +216,98 @@
     for k in (1, 2, 3):
         xa(k).wait_send()
 
-    partial[...] = jnp.zeros_like(partial)
     live = counts_ref[0]
 
     def slot_body(s, carry):
         q = cols_ref[s]
-        product = jnp.dot(
+        products[s] = jnp.dot(
             blocks_ref[s], panel[q // NZ, lax.rem(q, NZ)], preferred_element_type=jnp.float32
         )
-        for b in range(RB):
-            weight = jnp.where(jnp.logical_and(rows_ref[s] == b, s < live), 1.0, 0.0)
-            for part in range(NC):
-                partial[b, part] += weight * product[part * SHARE:(part + 1) * SHARE]
         return carry
 
     lax.fori_loop(0, 8, slot_body, 0)
 
-    pair = copy_to(partial.at[:, 1 - core], received, c_send, c_recv, r, y * NC + 1 - core)
-    pair.start()
-    pair.wait()
-    half[...] = partial[:, core] + received[...]
-    sends = []
-    for k in (1, 2, 3):
+    def pair(b):
+        return copy_to(
+            partial.at[b, 1 - core], received.at[b], c_send.at[b], c_recv.at[b], r, y * NC + 1 - core
+        )
+
+    def to_y(k):
         other = lax.rem(y + k, NY)
-        send = copy_to(
+        return copy_to(
             half.at[other], received2.at[k - 1], y_send.at[k - 1], y_recv.at[k - 1], r, other * NC + core
         )
-        send.start()
-        sends.append(send)
-    for send in sends:
-        send.wait()
+
+    def finish(k):
+        b = lax.rem(y + k, NY)
+        pair(b).wait_recv()
+        half[b] = partial[b, core] + received[b]
+        if k:
+            to_y(k).start()
+
+    order = (2, 1, 3, 0)
+    for place, k in enumerate(order):
+        b = lax.rem(y + k, NY)
+        for part in range(NC):
+            total = jnp.zeros((SHARE, WIDTH), jnp.float32)
+            for s in range(8):
+                weight = jnp.where(jnp.logical_and(rows_ref[s] == b, s < live), 1.0, 0.0)
+                total = total + weight * products[s, part * SHARE:(part + 1) * SHARE]
+            partial[b, part] = total
+        pair(b).start()
+        if place:
+            finish(order[place - 1])
+    finish(0)
+    for k in (1, 2, 3):
+        to_y(k).wait_recv()
     own = half[y] + received2[0] + received2[1] + received2[2]
     own_ref[...] = own
-    gram_ref[...] = lax.dot_general(
+    gram[...] = lax.dot_general(
         own, own, (((0,), (0,)), ((), ())), precision=HIGHEST, preferred_element_type=jnp.float32
-    )
-
-
-def sum_kernel(gram_ref, out_ref, slots, lines, a_send, a_recv, z_send, z_recv, b_send, b_recv):
-    r = lax.axis_index("rows")
-    c = lax.axis_index("cols")
-    x, z = r // NZ, lax.rem(r, NZ)
-    cols = NY * NC
-    me = x * cols + c
-
-    def member(k):
-        other = lax.rem(me + k, GROUP)
-        return other, (other // cols) * NZ + z, lax.rem(other, cols)
-
-    def along(k):
-        return x * NZ + lax.rem(z + k, NZ)
-
-    barrier = pltpu.get_barrier_semaphore()
-
-    def hello_group(k, carry):
-        _, row, col = member(k)
-        pl.semaphore_signal(barrier, inc=1, device_id=(row, col), device_id_type=MESH)
-        return carry
-
-    def hello_line(k, carry):
-        pl.semaphore_signal(barrier, inc=1, device_id=(along(k), c), device_id_type=MESH)
-        return carry
-
-    lax.fori_loop(1, GROUP, hello_group, 0)
-    lax.fori_loop(1, NZ, hello_line, 0)
-    pl.semaphore_wait(barrier, GROUP - 1 + NZ - 1)
+    ).reshape(GROUP, 8, WIDTH)
 
     def scatter(k):
         other, row, col = member(k)
-        return copy_to(gram_ref.at[other], slots.at[k - 1], a_send.at[k - 1], a_recv.at[k - 1], row, col)
-
-    def line(k):
-        return copy_to(lines.at[z], lines.at[z], z_send.at[k - 1], z_recv.at[k - 1], along(k), c)
-
-    def line_arrived(k):
-        source = lax.rem(z + NZ - k, NZ)
-        copy_to(
-            lines.at[source], lines.at[source], z_send.at[k - 1], z_recv.at[k - 1], along(k), c
-        ).wait_recv()
-
-    def spread(k):
+        return copy_to(gram.at[other], slots.at[k - 1], g_send.at[k - 1], g_recv.at[k - 1], row, col)
+
+    def near(k, source):
+        piece = lows.at[source]
+        return copy_to(piece, piece, l_send.at[k - 1], l_recv.at[k - 1], at_low(k), c)
+
+    def far(k, source):
+        piece = highs.at[source]
+        return copy_to(piece, piece, h_send.at[k - 1], h_recv.at[k - 1], at_high(k), c)
+
+    def spread(k, source):
         _, row, col = member(k)
-        return copy_to(out_ref.at[me], out_ref.at[me], b_send.at[k - 1], b_recv.at[k - 1], row, col)
-
-    def spread_arrived(k):
-        _, row, col = member(k)
-        source = lax.rem(me + GROUP - k, GROUP)
-        copy_to(
-            out_ref.at[source], out_ref.at[source], b_send.at[k - 1], b_recv.at[k - 1], row, col
-        ).wait_recv()
-
-    def loop(start, stop, act):
+        piece = gram_ref.at[source]
+        return copy_to(piece, piece, s_send.at[k - 1], s_recv.at[k - 1], row, col)
+
+    def each(stop, act):
         def body(k, carry):
             act(k)
             return carry
-        lax.fori_loop(start, stop, body, 0)
-
-    loop(1, GROUP, lambda k: scatter(k).start())
-    loop(1, GROUP, lambda k: scatter(k).wait())
-    lines[z] = gram_ref[me] + jnp.sum(slots[...], axis=0)
-    loop(1, NZ, lambda k: line(k).start())
-    loop(1, NZ, line_arrived)
-    out_ref[me] = jnp.sum(lines[...], axis=0)
-    loop(1, GROUP, lambda k: spread(k).start())
-    loop(1, GROUP, spread_arrived)
-    loop(1, NZ, lambda k: line(k).wait_send())
-    loop(1, GROUP, lambda k: spread(k).wait_send())
+        lax.fori_loop(1, stop, body, 0)
+
+    each(GROUP, lambda k: scatter(k).start())
+    each(GROUP, lambda k: scatter(k).wait_recv())
+    lows[low] = gram[me] + jnp.sum(slots[...], axis=0)
+    each(LINE, lambda k: near(k, low).start())
+    each(LINE, lambda k: near(k, lax.rem(low + LINE - k, LINE)).wait_recv())
+    highs[high] = jnp.sum(lows[...], axis=0)
+    each(LINE, lambda k: far(k, high).start())
+    each(LINE, lambda k: far(k, lax.rem(high + LINE - k, LINE)).wait_recv())
+    gram_ref[me] = jnp.sum(highs[...], axis=0)
+    each(GROUP, lambda k: spread(k, me).start())
+    for k in range(NY):
+        pair(k).wait_send()
+    for k in (1, 2, 3):
+        to_y(k).wait_send()
+    each(GROUP, lambda k: scatter(k).wait_send())
+    each(LINE, lambda k: near(k, low).wait_send())
+    each(LINE, lambda k: far(k, high).wait_send())
+    each(GROUP, lambda k: spread(k, lax.rem(me + GROUP - k, GROUP)).wait_recv())
+    each(GROUP, lambda k: spread(k, me).wait_send())
 
 
 def factor_kernel(step, root, gram_ref, own_ref, basis_ref, factor_ref, work, rows):
@@ -391,43 +397,38 @@
         sketch_kernel,
         out_shape=(
             jax.ShapeDtypeStruct((SHARE, WIDTH), f32),
-            jax.ShapeDtypeStruct((WIDTH, WIDTH), f32),
+            jax.ShapeDtypeStruct((GROUP, 8, WIDTH), f32),
         ),
         in_specs=[smem, smem, smem, vmem, vmem],
         out_specs=(vmem, vmem),
         scratch_shapes=[
             pltpu.VMEM((NX, NZ, WIDTH, WIDTH), jnp.bfloat16),
+            pltpu.VMEM((8, WIDTH, WIDTH), f32),
             pltpu.VMEM((RB, NC, SHARE, WIDTH), f32),
             pltpu.VMEM((RB, SHARE, WIDTH), f32),
             pltpu.VMEM((RB, SHARE, WIDTH), f32),
             pltpu.VMEM((NY - 1, SHARE, WIDTH), f32),
+            pltpu.VMEM((GROUP, 8, WIDTH), f32),
+            pltpu.VMEM((GROUP - 1, 8, WIDTH), f32),
+            pltpu.VMEM((LINE, 8, WIDTH), f32),
+            pltpu.VMEM((LINE, 8, WIDTH), f32),
             dma,
             dma((3,)), dma((3,)),
             dma((2, 8)), dma((2, 8)),
             dma((2, 8)), dma((2, 8)),
             dma((2, 2, 8)), dma((2, 2, 8)),
             dma((2, 8)), dma((2, 8)),
-            dma, dma,
+            dma((4,)), dma((4,)),
             dma((3,)), dma((3,)),
+            dma((GROUP - 1,)), dma((GROUP - 1,)),
+            dma((3,)), dma((3,)),
+            dma((3,)), dma((3,)),
+            dma((GROUP - 1,)), dma((GROUP - 1,)),
         ],
         compiler_params=pltpu.CompilerParams(collective_id=0, has_side_effects=True),
         name="sketch",
     )(block_rows, block_cols, counts, sketch, blocks)
-    gram = pl.pallas_call(
-        sum_kernel,
-        out_shape=jax.ShapeDtypeStruct((GROUP, 8, WIDTH), f32),
-        in_specs=[vmem],
-        out_specs=vmem,
-        scratch_shapes=[
-            pltpu.VMEM((GROUP - 1, 8, WIDTH), f32),
-            pltpu.VMEM((NZ, 8, WIDTH), f32),
-            dma((GROUP - 1,)), dma((GROUP - 1,)),
-            dma((NZ - 1,)), dma((NZ - 1,)),
-            dma((GROUP - 1,)), dma((GROUP - 1,)),
-        ],
-        compiler_params=pltpu.CompilerParams(collective_id=1, has_side_effects=True),
-        name="gram_sum",
-    )(gram.reshape(GROUP, 8, WIDTH)).reshape(WIDTH, WIDTH)
+    gram = gram.reshape(WIDTH, WIDTH)
     return factorize(gram, own, 4)
 
 

time: 135 us -> 126 us (0.933)
  Pallas kernels: 133 us -> 124 us
    pallas_call x1 -> x0, Pallas kernels: 32.4 us -> none  [local(): pl.pallas_call(sum_kernel, out_shape=jax.ShapeDtypeStruct((GROUP, 8, WIDT...]
    pallas_call x1, Pallas kernels: 87.3 us -> 111 us  [local(): pl.pallas_call(sketch_kernel, out_shape=(jax.ShapeDtypeStruct((SHARE, WID...]
where the time goes in v3:
time: 126 us
  Pallas kernels  124 us (98%)
  between operations  1.29 us (1%)
    pallas_call x1, Pallas kernels, local(): pl.pallas_call(sketch_kernel, out_shape=(jax.ShapeDtypeStruct((SHARE, WID...  111 us
    pallas_call x1, Pallas kernels, factorize(): pl.pallas_call(functools.partial(factor_kernel, step, root), out_shape=(j...  13.8 us

profile of v3, /device:TPU:1, one launch (start us, length us, event | category | flops | bytes accessed | tf_op | source)
XLA Modules:
  0.0 125.6 jit_solution(10273515930994670504)
XLA Ops:
  1.3 110.5 %sketch.1 = (f32[128,256]{1,0:T(8,128)}, f32[32,8,256]{2,1,0:T(8,128)}) custom-call(s32[8]{0:T(128)} %rows_ref.1, s32[8]{0:T(128)} %cols_ref.1, s32[1]{0:T(128)S(6)} %copy.7.counts_ref, bf16[256,256]{1,0:T(8,128)(2,1)} %sketch_ref.1, bf16[8,256,256]{2,1,0:T(8,128)(2,1)} %blocks_ref.1), custom_call_target="tpu_custom_call" | custom-call | tf_op jit(solution)/shard_map/sketch/pallas_call | solution.py:396
  111.8 13.8 %factorize.1 = (f32[128,256]{1,0:T(8,128)}, f32[256,256]{1,0:T(8,128)}) custom-call(f32[256,256]{1,0:T(8,128)} %bitcast.1, f32[128,256]{1,0:T(8,128)} %get-tuple-element.5.own_ref), custom_call_target="tpu_custom_call" | custom-call | tf_op jit(solution)/shard_map/factorize/pallas_call | solution.py:378

commit v4 on v3

--- a/solution.py
+++ b/solution.py
@@ -13,7 +13,7 @@
 NX, NZ, NY, NC = 4, 16, 4, 2
 WIDTH = 256
 SPLIT = 80
-GROUP, LINE = 32, 4
+GROUP = 32
 SHARE = 128
 HALF = 128
 
@@ -27,10 +27,10 @@
 
 def sketch_kernel(
     rows_ref, cols_ref, counts_ref, sketch_ref, blocks_ref, own_ref, gram_ref,
-    panel, products, partial, received, half, received2, gram, slots, lows, highs,
+    panel, products, partial, received, half, received2, gram, slots, lows,
     local_sem, xa_send, xa_recv, za_send, za_recv, zb_send, zb_recv,
     xb_send, xb_recv, op_send, op_recv, c_send, c_recv, y_send, y_recv,
-    g_send, g_recv, l_send, l_recv, h_send, h_recv, s_send, s_recv,
+    g_send, g_recv, l_send, l_recv, s_send, s_recv,
 ):
     r = lax.axis_index("rows")
     c = lax.axis_index("cols")
@@ -45,39 +45,25 @@
 
     cols = NY * NC
     me = x * cols + c
-    low, high = lax.rem(z, LINE), z // LINE
 
     def member(k):
         other = lax.rem(me + k, GROUP)
         return other, (other // cols) * NZ + z, lax.rem(other, cols)
 
-    def at_low(k):
-        return x * NZ + high * LINE + lax.rem(low + k, LINE)
-
-    def at_high(k):
-        return x * NZ + lax.rem(high + k, LINE) * LINE + low
-
     barrier = pltpu.get_barrier_semaphore()
 
     def hello(row, col):
         pl.semaphore_signal(barrier, inc=1, device_id=(row, col), device_id_type=MESH)
 
-    def hello_group(k, carry):
-        _, row, col = member(k)
-        hello(row, col)
-        return carry
-
-    for row in (at_z(1), at_z(NZ - 1)):
+    for row in (at_z(1), at_z(NZ - 1), at_x(1), at_x(2), at_x(3)):
         hello(row, c)
-    for k in range(1, LINE):
-        hello(at_low(k), c)
-        hello(at_high(k), c)
-    lax.fori_loop(1, GROUP, hello_group, 0)
-    pl.semaphore_wait(barrier, 2 + 2 * (LINE - 1) + GROUP - 1)
+    hello(r, y * NC + 1 - core)
+    for k in (1, 2, 3):
+        hello(r, lax.rem(y + k, NY) * NC + core)
+    pl.semaphore_wait(barrier, 9)
 
     local = pltpu.make_async_copy(sketch_ref, panel.at[x, z], local_sem)
     local.start()
-    local.wait()
 
     first = pl.ds(0, SPLIT)
     second = pl.ds(SPLIT, WIDTH - SPLIT)
@@ -87,7 +73,7 @@
 
     def xa(k):
         piece = panel.at[x, z, first]
-        return copy_to(piece, piece, xa_send.at[k - 1], xa_recv.at[k - 1], at_x(k), c)
+        return copy_to(sketch_ref.at[first], piece, xa_send.at[k - 1], xa_recv.at[k - 1], at_x(k), c)
 
     def za(side, hop):
         step = 1 - 2 * side
@@ -141,6 +127,7 @@
 
     for k in (1, 2, 3):
         xa(k).start()
+    local.wait()
     for side in (0, 1):
         zb(side, 1).start()
     for way in (0, 1):
@@ -270,13 +257,10 @@
         other, row, col = member(k)
         return copy_to(gram.at[other], slots.at[k - 1], g_send.at[k - 1], g_recv.at[k - 1], row, col)
 
-    def near(k, source):
-        piece = lows.at[source]
-        return copy_to(piece, piece, l_send.at[k - 1], l_recv.at[k - 1], at_low(k), c)
-
-    def far(k, source):
-        piece = highs.at[source]
-        return copy_to(piece, piece, h_send.at[k - 1], h_recv.at[k - 1], at_high(k), c)
+    def line(i, source):
+        hops = 8 - i // 2
+        k = lax.rem(i, 2) * (NZ - 2 * hops) + hops
+        return copy_to(lows.at[source(k)], lows.at[source(k)], l_send.at[i], l_recv.at[i], at_z(k), c)
 
     def spread(k, source):
         _, row, col = member(k)
@@ -291,21 +275,23 @@
 
     each(GROUP, lambda k: scatter(k).start())
     each(GROUP, lambda k: scatter(k).wait_recv())
-    lows[low] = gram[me] + jnp.sum(slots[...], axis=0)
-    each(LINE, lambda k: near(k, low).start())
-    each(LINE, lambda k: near(k, lax.rem(low + LINE - k, LINE)).wait_recv())
-    highs[high] = jnp.sum(lows[...], axis=0)
-    each(LINE, lambda k: far(k, high).start())
-    each(LINE, lambda k: far(k, lax.rem(high + LINE - k, LINE)).wait_recv())
-    gram_ref[me] = jnp.sum(highs[...], axis=0)
+    def along(act):
+        def body(i, carry):
+            act(i)
+            return carry
+        lax.fori_loop(1, NZ, body, 0)
+
+    lows[z] = gram[me] + jnp.sum(slots[...], axis=0)
+    along(lambda i: line(i, lambda k: z).start())
+    along(lambda i: line(i, lambda k: lax.rem(z + NZ - k, NZ)).wait_recv())
+    gram_ref[me] = jnp.sum(lows[...], axis=0)
     each(GROUP, lambda k: spread(k, me).start())
     for k in range(NY):
         pair(k).wait_send()
     for k in (1, 2, 3):
         to_y(k).wait_send()
     each(GROUP, lambda k: scatter(k).wait_send())
-    each(LINE, lambda k: near(k, low).wait_send())
-    each(LINE, lambda k: far(k, high).wait_send())
+    along(lambda i: line(i, lambda k: z).wait_send())
     each(GROUP, lambda k: spread(k, lax.rem(me + GROUP - k, GROUP)).wait_recv())
     each(GROUP, lambda k: spread(k, me).wait_send())
 
@@ -410,8 +396,7 @@
             pltpu.VMEM((NY - 1, SHARE, WIDTH), f32),
             pltpu.VMEM((GROUP, 8, WIDTH), f32),
             pltpu.VMEM((GROUP - 1, 8, WIDTH), f32),
-            pltpu.VMEM((LINE, 8, WIDTH), f32),
-            pltpu.VMEM((LINE, 8, WIDTH), f32),
+            pltpu.VMEM((NZ, 8, WIDTH), f32),
             dma,
             dma((3,)), dma((3,)),
             dma((2, 8)), dma((2, 8)),
@@ -421,8 +406,7 @@
             dma((4,)), dma((4,)),
             dma((3,)), dma((3,)),
             dma((GROUP - 1,)), dma((GROUP - 1,)),
-            dma((3,)), dma((3,)),
-            dma((3,)), dma((3,)),
+            dma((NZ,)), dma((NZ,)),
             dma((GROUP - 1,)), dma((GROUP - 1,)),
         ],
         compiler_params=pltpu.CompilerParams(collective_id=0, has_side_effects=True),

time: 126 us -> 122 us (0.968)
  Pallas kernels: 124 us -> 121 us
    pallas_call x1, Pallas kernels: 111 us -> 107 us  [local(): pl.pallas_call(sketch_kernel, out_shape=(jax.ShapeDtypeStruct((SHARE, WID...]
where the time goes in v4:
time: 122 us
  Pallas kernels  121 us (99%)
  between operations  1.29 us (1%)
    pallas_call x1, Pallas kernels, local(): pl.pallas_call(sketch_kernel, out_shape=(jax.ShapeDtypeStruct((SHARE, WID...  107 us
    pallas_call x1, Pallas kernels, factorize(): pl.pallas_call(functools.partial(factor_kernel, step, root), out_shape=(j...  13.8 us

profile of v4, /device:TPU:1, one launch (start us, length us, event | category | flops | bytes accessed | tf_op | source)
XLA Modules:
  0.0 122.3 jit_solution(8261040800255886729)
XLA Ops:
  1.3 107.2 %sketch.1 = (f32[128,256]{1,0:T(8,128)}, f32[32,8,256]{2,1,0:T(8,128)}) custom-call(s32[8]{0:T(128)} %rows_ref.1, s32[8]{0:T(128)} %cols_ref.1, s32[1]{0:T(128)S(6)} %copy.7.counts_ref, bf16[256,256]{1,0:T(8,128)(2,1)} %sketch_ref.1, bf16[8,256,256]{2,1,0:T(8,128)(2,1)} %blocks_ref.1), custom_call_target="tpu_custom_call" | custom-call | tf_op jit(solution)/shard_map/sketch/pallas_call | solution.py:382
  108.5 13.8 %factorize.1 = (f32[128,256]{1,0:T(8,128)}, f32[256,256]{1,0:T(8,128)}) custom-call(f32[256,256]{1,0:T(8,128)} %bitcast.1, f32[128,256]{1,0:T(8,128)} %get-tuple-element.5.own_ref), custom_call_target="tpu_custom_call" | custom-call | tf_op jit(solution)/shard_map/factorize/pallas_call | solution.py:364

commit v5 on v4

--- a/solution.py
+++ b/solution.py
@@ -15,7 +15,7 @@
 SPLIT = 80
 GROUP = 32
 SHARE = 128
-HALF = 128
+BLOCK = 64
 
 
 def copy_to(src, dst, send_sem, recv_sem, row, col):
@@ -298,14 +298,11 @@
 
 def factor_kernel(step, root, gram_ref, own_ref, basis_ref, factor_ref, work, rows):
     f32 = jnp.float32
-    lane = lax.broadcasted_iota(jnp.int32, (1, HALF), 1)
-    below = lax.broadcasted_iota(jnp.int32, (HALF, HALF), 0) > lax.broadcasted_iota(
-        jnp.int32, (HALF, HALF), 1
-    )
-    eye = (
-        lax.broadcasted_iota(jnp.int32, (HALF, HALF), 0)
-        == lax.broadcasted_iota(jnp.int32, (HALF, HALF), 1)
-    ).astype(f32)
+    lane = lax.broadcasted_iota(jnp.int32, (1, 2 * BLOCK), 1)
+    row_index = lax.broadcasted_iota(jnp.int32, (BLOCK, BLOCK), 0)
+    lane_index = lax.broadcasted_iota(jnp.int32, (BLOCK, BLOCK), 1)
+    below = row_index > lane_index
+    eye = (row_index == lane_index).astype(f32)
 
     def dot(a, b, dims):
         return lax.dot_general(a, b, (dims, ((), ())), precision=HIGHEST, preferred_element_type=f32)
@@ -314,14 +311,13 @@
         return jnp.sum(jnp.where(lane == j, value, 0.0), axis=1, keepdims=True)
 
     def eliminate(block):
-        work[:, :HALF] = block
-        work[:, HALF:] = eye
+        work[...] = jnp.concatenate([block, eye], axis=1)
 
         def body(i, carry):
             j = i * step
             line = [work[pl.ds(j + t, 1), :] for t in range(step)]
-            column = [pick(work[:, :HALF], j + t) for t in range(step)]
-            entry = [[pick(line[t][:, :HALF], j + u) for u in range(step)] for t in range(step)]
+            column = [pick(work[...], j + t) for t in range(step)]
+            entry = [[pick(line[t], j + u) for u in range(step)] for t in range(step)]
             scaled = []
             for t in range(step):
                 inverse = 1.0 / entry[t][t]
@@ -340,21 +336,23 @@
                 rows[pl.ds(j + t, 1), :] = line[t] * (1.0 / jnp.sqrt(entry[t][t]))
             return carry
 
-        lax.fori_loop(0, HALF // step, body, 0)
-        return jnp.where(below, 0.0, rows[:, :HALF]), rows[:, HALF:]
-
-    upper1, inverse1 = eliminate(gram_ref[:HALF, :HALF])
-    cross = dot(inverse1, gram_ref[:HALF, HALF:], ((1,), (0,)))
-    factor_ref[:HALF, :HALF] = upper1 * (1.0 / root)
-    factor_ref[:HALF, HALF:] = cross * (1.0 / root)
-    factor_ref[HALF:, :HALF] = jnp.zeros((HALF, HALF), f32)
-    solved = dot(own_ref[:, :HALF], inverse1, ((1,), (1,)))
-    basis_ref[:, :HALF] = solved * root
-    rest = own_ref[:, HALF:] - dot(solved, cross, ((1,), (0,)))
-    schur = gram_ref[HALF:, HALF:] - dot(cross, cross, ((0,), (0,)))
-    upper2, inverse2 = eliminate(schur)
-    factor_ref[HALF:, HALF:] = upper2 * (1.0 / root)
-    basis_ref[:, HALF:] = dot(rest, inverse2, ((1,), (1,))) * root
+        lax.fori_loop(0, BLOCK // step, body, 0)
+        return jnp.where(below, 0.0, rows[:, :BLOCK]), rows[:, BLOCK:]
+
+    rest, share = gram_ref[...], own_ref[...]
+    for first in range(0, WIDTH, BLOCK):
+        last = first + BLOCK
+        upper, inverse = eliminate(rest[:BLOCK, :BLOCK])
+        factor_ref[first:last, first:last] = upper * (1.0 / root)
+        if first:
+            factor_ref[first:last, :first] = jnp.zeros((BLOCK, first), f32)
+        solved = dot(share[:, :BLOCK], inverse, ((1,), (1,)))
+        basis_ref[:, first:last] = solved * root
+        if last < WIDTH:
+            cross = dot(inverse, rest[:BLOCK, BLOCK:], ((1,), (0,)))
+            factor_ref[first:last, last:] = cross * (1.0 / root)
+            share = share[:, BLOCK:] - dot(solved, cross, ((1,), (0,)))
+            rest = rest[BLOCK:, BLOCK:] - dot(cross, cross, ((0,), (0,)))
 
 
 def factorize(gram, own, step):
@@ -369,7 +367,7 @@
         ),
         in_specs=[vmem, vmem],
         out_specs=(vmem, vmem),
-        scratch_shapes=[pltpu.VMEM((HALF, WIDTH), f32), pltpu.VMEM((HALF, WIDTH), f32)],
+        scratch_shapes=[pltpu.VMEM((BLOCK, 2 * BLOCK), f32), pltpu.VMEM((BLOCK, 2 * BLOCK), f32)],
         name="factorize",
     )(gram, own)
 
@@ -413,7 +411,7 @@
         name="sketch",
     )(block_rows, block_cols, counts, sketch, blocks)
     gram = gram.reshape(WIDTH, WIDTH)
-    return factorize(gram, own, 4)
+    return factorize(gram, own, 8)
 
 
 def solution(mesh):

time: 122 us -> 120 us (0.984)
  Pallas kernels: 121 us -> 119 us
    pallas_call x1, Pallas kernels: 13.8 us -> 11.3 us  [factorize(): pl.pallas_call(functools.partial(factor_kernel, step, root), out_shape=(j...]
where the time goes in v5:
time: 120 us
  Pallas kernels  119 us (99%)
  between operations  1.29 us (1%)
    pallas_call x1, Pallas kernels, local(): pl.pallas_call(sketch_kernel, out_shape=(jax.ShapeDtypeStruct((SHARE, WID...  107 us
    pallas_call x1, Pallas kernels, factorize(): pl.pallas_call(functools.partial(factor_kernel, step, root), out_shape=(j...  11.3 us

profile of v5, /device:TPU:1, one launch (start us, length us, event | category | flops | bytes accessed | tf_op | source)
XLA Modules:
  0.0 119.8 jit_solution(8938162549019772726)
XLA Ops:
  1.3 107.2 %sketch.1 = (f32[128,256]{1,0:T(8,128)}, f32[32,8,256]{2,1,0:T(8,128)}) custom-call(s32[8]{0:T(128)} %rows_ref.1, s32[8]{0:T(128)} %cols_ref.1, s32[1]{0:T(128)S(6)} %copy.7.counts_ref, bf16[256,256]{1,0:T(8,128)(2,1)} %sketch_ref.1, bf16[8,256,256]{2,1,0:T(8,128)(2,1)} %blocks_ref.1), custom_call_target="tpu_custom_call" | custom-call | tf_op jit(solution)/shard_map/sketch/pallas_call | solution.py:380
  108.5 11.3 %factorize.1 = (f32[128,256]{1,0:T(8,128)}, f32[256,256]{1,0:T(8,128)}) custom-call(f32[256,256]{1,0:T(8,128)} %bitcast.1, f32[128,256]{1,0:T(8,128)} %get-tuple-element.5.own_ref), custom_call_target="tpu_custom_call" | custom-call | tf_op jit(solution)/shard_map/factorize/pallas_call | solution.py:362

commit v6 on v5

--- a/solution.py
+++ b/solution.py
@@ -181,27 +181,14 @@
     op(0, 7).start()
     za_arrived(1, 8)
 
-    def drain(slot, carry):
+    def arrived(slot, carry):
         xb_arrived(0, slot, 1)
         xb_arrived(1, slot, 0)
         for family in (0, 1):
             op_arrived(family, slot)
-            op(family, slot).wait_send()
-            for way in (0, 1):
-                xb(family, slot, way).wait_send()
-        zb(0, slot + 1).wait_send()
-        za(1, slot + 1).wait_send()
-
-        @pl.when(slot < 7)
-        def _():
-            zb(1, slot + 1).wait_send()
-            za(0, slot + 1).wait_send()
-
         return carry
 
-    lax.fori_loop(0, 8, drain, 0)
-    for k in (1, 2, 3):
-        xa(k).wait_send()
+    lax.fori_loop(0, 8, arrived, 0)
 
     live = counts_ref[0]
 
@@ -286,6 +273,25 @@
     along(lambda i: line(i, lambda k: lax.rem(z + NZ - k, NZ)).wait_recv())
     gram_ref[me] = jnp.sum(lows[...], axis=0)
     each(GROUP, lambda k: spread(k, me).start())
+
+    def drain(slot, carry):
+        for family in (0, 1):
+            op(family, slot).wait_send()
+            for way in (0, 1):
+                xb(family, slot, way).wait_send()
+        zb(0, slot + 1).wait_send()
+        za(1, slot + 1).wait_send()
+
+        @pl.when(slot < 7)
+        def _():
+            zb(1, slot + 1).wait_send()
+            za(0, slot + 1).wait_send()
+
+        return carry
+
+    lax.fori_loop(0, 8, drain, 0)
+    for k in (1, 2, 3):
+        xa(k).wait_send()
     for k in range(NY):
         pair(k).wait_send()
     for k in (1, 2, 3):

time: 120 us -> 120 us (level)
  no operation moved by 1% of the time
where the time goes in v6:
time: 120 us
  Pallas kernels  119 us (99%)
  between operations  1.29 us (1%)
    pallas_call x1, Pallas kernels, local(): pl.pallas_call(sketch_kernel, out_shape=(jax.ShapeDtypeStruct((SHARE, WID...  107 us
    pallas_call x1, Pallas kernels, factorize(): pl.pallas_call(functools.partial(factor_kernel, step, root), out_shape=(j...  11.3 us

profile of v6, /device:TPU:1, one launch (start us, length us, event | category | flops | bytes accessed | tf_op | source)
XLA Modules:
  0.0 119.8 jit_solution(17462811358192817506)
XLA Ops:
  1.3 107.2 %sketch.1 = (f32[128,256]{1,0:T(8,128)}, f32[32,8,256]{2,1,0:T(8,128)}) custom-call(s32[8]{0:T(128)} %rows_ref.1, s32[8]{0:T(128)} %cols_ref.1, s32[1]{0:T(128)S(6)} %copy.7.counts_ref, bf16[256,256]{1,0:T(8,128)(2,1)} %sketch_ref.1, bf16[8,256,256]{2,1,0:T(8,128)(2,1)} %blocks_ref.1), custom_call_target="tpu_custom_call" | custom-call | tf_op jit(solution)/shard_map/sketch/pallas_call | solution.py:386
  108.5 11.3 %factorize.1 = (f32[128,256]{1,0:T(8,128)}, f32[256,256]{1,0:T(8,128)}) custom-call(f32[256,256]{1,0:T(8,128)} %bitcast.1, f32[128,256]{1,0:T(8,128)} %get-tuple-element.5.own_ref), custom_call_target="tpu_custom_call" | custom-call | tf_op jit(solution)/shard_map/factorize/pallas_call | solution.py:368
